TPU v7x, 32 devices: a whole 2x2x4 slice. The times are simulated.
32 devices in a mesh: shard: 4 (over y, x), ctx: 2 (over core), tp: 4 (over z).
Axes of the slice: x: 2, y: 2, z: 4, core: 2. Of those that a mesh axis runs over, the one named last changes fastest.
Arguments:
- tokens: bfloat16 [4, 1024, 1536], P('shard', ('ctx', 'tp')), may hold values from -6 to 6
- cotangent: bfloat16 [4, 1024, 1536], P('shard', ('ctx', 'tp')), may hold values from -6 to 6
- lengths: int32 [4], P('shard'), may hold values from 256 to 1024, as said below
- w_qkv: bfloat16 [1536, 3, 1536], P(('shard', 'ctx'), None, 'tp'), may hold values from -0.15625 to 0.15625
- w_forget: bfloat16 [1536, 24], P(('shard', 'ctx'), 'tp'), may hold values from -0.15625 to 0.15625
- forget_bias: float32 [24], replicated, may hold values from 3 to 8
- w_ogate: bfloat16 [1536, 1536], P(('shard', 'ctx'), 'tp'), may hold values from -0.15625 to 0.15625
- w_out: bfloat16 [1536, 1536], P(('shard', 'ctx'), 'tp'), may hold values from -0.625 to 0.625
- w_gu: bfloat16 [1536, 2, 4096], P(('shard', 'ctx'), None, 'tp'), may hold values from -0.15625 to 0.15625
- w_down: bfloat16 [1536, 4096], P(('shard', 'ctx'), 'tp'), may hold values from -0.09375 to 0.09375
- gain_attn: float32 [1536], replicated, may hold values from 0.5 to 1.5
- gain_mlp: float32 [1536], replicated, may hold values from 0.5 to 1.5
- qk_gain: float32 [2, 64], replicated, may hold values from 1 to 2
Outputs:
- output: bfloat16 [4, 1024, 1536], P('shard', ('ctx', 'tp'))
- input_grad: bfloat16 [4, 1024, 1536], P('shard', ('ctx', 'tp'))
- grad_qkv: float32 [1536, 3, 1536], P(('shard', 'ctx'), None, 'tp')
- grad_forget: float32 [1536, 24], P(('shard', 'ctx'), 'tp')
- grad_forget_bias: float32 [24], replicated
- grad_ogate: float32 [1536, 1536], P(('shard', 'ctx'), 'tp')
- grad_out: float32 [1536, 1536], P(('shard', 'ctx'), 'tp')
- grad_gu: float32 [1536, 2, 4096], P(('shard', 'ctx'), None, 'tp')
- grad_down: float32 [1536, 4096], P(('shard', 'ctx'), 'tp')
- grad_gain_attn: float32 [1536], replicated
- grad_gain_mlp: float32 [1536], replicated
- grad_qk_gain: float32 [2, 64], replicated
Inputs may be any that keep to these rules, and one draw needn't show every extreme that they name: `lengths`: real tokens of a slot; positions at or past it are padding; both the least and the most value occur in every draw.
All inputs are finite; a program needn't handle non-finite values.
Results may differ from a plain program's by a relative error of at most 0.04.
Values may be sent and summed in bfloat16 or wider, within the bound.
No kernel may reach another device: no remote copies, remote signals or barrier semaphores. Data moves between devices by JAX's collectives and lax.ppermute only.
A program may use at most 128 MiB of HBM per device.

v0:
```python
import math
import jax
import jax.numpy as jnp
from jax import lax
from jax.sharding import PartitionSpec as P

epsilon = 1e-06


def shifted(block, axis, distance):
    devices = range(lax.axis_size(axis))
    route = [(i - distance, i) for i in devices if i - distance in devices]
    return lax.ppermute(block, axis, route)


def norm_rows(values, gain):
    return values * lax.rsqrt(jnp.mean(values * values, axis=-1, keepdims=True) + epsilon) * gain


def product(left, right):
    return jnp.dot(left, right, preferred_element_type=jnp.float32)


def product_t(left, right):
    return lax.dot_general(
        left, right, (((1,), (1,)), ((), ())), preferred_element_type=jnp.float32
    )


def outer_rows(left, right):
    return lax.dot_general(
        left, right, (((0,), (0,)), ((), ())), preferred_element_type=jnp.float32
    )


def body(
    tokens,
    cotangent,
    lengths,
    w_qkv,
    w_forget,
    forget_bias,
    w_ogate,
    w_out,
    w_gu,
    w_down,
    gain_attn,
    gain_mlp,
    qk_gain,
):
    slot_count, own_rows, model_width = tokens.shape
    tensor_size = lax.axis_size("tp")
    tensor_place = lax.axis_index("tp")
    span_index = lax.axis_index("ctx")
    half_rows = own_rows * tensor_size
    row_count = slot_count * half_rows
    local_heads = w_forget.shape[1]
    head_size = qk_gain.shape[1]
    head_cols = local_heads * head_size
    hidden_units = w_down.shape[1]
    item_count = slot_count * local_heads
    score_scale = 1.0 / math.sqrt(head_size)
    own_start = tensor_place * own_rows
    full_tokens, full_cot = (
        lax.all_gather(tokens, "tp", axis=1, tiled=True),
        lax.all_gather(cotangent, "tp", axis=1, tiled=True),
    )
    qkv_full, forget_full, ogate_full, out_full, gu_full, down_full = (
        lax.all_gather(w_qkv, ("shard", "ctx"), axis=0, tiled=True),
        lax.all_gather(w_forget, ("shard", "ctx"), axis=0, tiled=True),
        lax.all_gather(w_ogate, ("shard", "ctx"), axis=0, tiled=True),
        lax.all_gather(w_out, ("shard", "ctx"), axis=0, tiled=True),
        lax.all_gather(w_gu, ("shard", "ctx"), axis=0, tiled=True),
        lax.all_gather(w_down, ("shard", "ctx"), axis=0, tiled=True),
    )
    qkv_flat = qkv_full.reshape(model_width, 3 * head_cols)
    gu_flat = gu_full.reshape(model_width, 2 * hidden_units)

    def own_slice(values):
        return lax.dynamic_slice_in_dim(
            values.reshape(slot_count, half_rows, values.shape[-1]), own_start, own_rows, 1
        )

    positions = span_index * half_rows + jnp.arange(half_rows, dtype=jnp.int32)
    valid_rows = (positions[None, :] < lengths[:, None]).astype(jnp.float32).reshape(row_count, 1)
    own_positions = span_index * half_rows + own_start + jnp.arange(own_rows, dtype=jnp.int32)
    valid_own = (own_positions[None, :] < lengths[:, None]).astype(jnp.float32)[:, :, None]
    residual = full_tokens.reshape(row_count, model_width).astype(jnp.float32)
    normed = norm_rows(residual, gain_attn).astype(jnp.bfloat16)
    qkv_rows = product(normed, qkv_flat).reshape(row_count, 3, head_cols)
    query_raw = qkv_rows[:, 0].reshape(row_count, local_heads, head_size)
    key_raw = qkv_rows[:, 1].reshape(row_count, local_heads, head_size)
    queries = (
        norm_rows(query_raw, qk_gain[0])
        .astype(jnp.bfloat16)
        .reshape(slot_count, half_rows, head_cols)
    )
    keys_here = (
        norm_rows(key_raw, qk_gain[1])
        .astype(jnp.bfloat16)
        .reshape(slot_count, half_rows, head_cols)
    )
    values_here = qkv_rows[:, 2].astype(jnp.bfloat16).reshape(slot_count, half_rows, head_cols)
    bias_here = lax.dynamic_slice_in_dim(forget_bias, tensor_place * local_heads, local_heads)
    forget_pre = (product(normed, forget_full) + bias_here).reshape(
        slot_count, half_rows, local_heads
    )
    cum_here = jnp.cumsum(jax.nn.log_sigmoid(forget_pre), axis=1)
    keys_left, values_left = shifted((keys_here, values_here), "ctx", 1)
    cum_left = shifted(cum_here, "ctx", 1)
    cum_query = cum_here + cum_left[:, -1:, :]

    def by_head(values):
        shaped = values.reshape(slot_count, half_rows, local_heads, head_size)
        return jnp.transpose(shaped, (0, 2, 1, 3)).reshape(item_count, half_rows, head_size)

    def by_head_cum(values):
        return jnp.transpose(values, (0, 2, 1)).reshape(item_count, half_rows)

    def to_slots(values):
        shaped = values.reshape(slot_count, local_heads, half_rows, head_size)
        return jnp.transpose(shaped, (0, 2, 1, 3)).reshape(slot_count, half_rows, head_cols)

    def to_slots_cum(values):
        return jnp.transpose(values.reshape(slot_count, local_heads, half_rows), (0, 2, 1))

    q_items = by_head(queries)
    k_items = jnp.concatenate([by_head(keys_left), by_head(keys_here)], axis=1)
    v_items = jnp.concatenate([by_head(values_left), by_head(values_here)], axis=1)
    cq_items = by_head_cum(cum_query)
    ck_items = jnp.concatenate([by_head_cum(cum_left), cq_items], axis=1)
    place_ids = jnp.arange(half_rows, dtype=jnp.int32)
    earlier = jnp.broadcast_to(span_index > 0, (half_rows, half_rows))
    allowed = jnp.concatenate([earlier, place_ids[None, :] <= place_ids[:, None]], axis=1)

    def score_block(query_block, key_block, cum_rows, cum_cols):
        score_raw = (
            product_t(query_block, key_block) * score_scale + cum_rows[:, None] - cum_cols[None, :]
        )
        return jnp.where(allowed, score_raw, -jnp.inf)

    def forward_item(pieces):
        query_block, key_block, value_block, cum_rows, cum_cols = pieces
        score_vals = score_block(query_block, key_block, cum_rows, cum_cols)
        row_max = jnp.max(score_vals, axis=1, keepdims=True)
        expo = jnp.exp(score_vals - row_max)
        row_total = jnp.sum(expo, axis=1, keepdims=True)
        attn_probs = (expo / row_total).astype(jnp.bfloat16)
        return (product(attn_probs, value_block), (row_max + jnp.log(row_total))[:, 0])

    attended_items, lse_items = lax.map(
        forward_item, (q_items, k_items, v_items, cq_items, ck_items)
    )
    attended_rows = to_slots(attended_items).reshape(row_count, head_cols)
    opener = jax.nn.sigmoid(product(normed, ogate_full))
    gated = (attended_rows * opener).astype(jnp.bfloat16)
    branch_part = product_t(gated, out_full)
    branch_full = lax.psum(branch_part, "tp")
    middle = residual + branch_full
    middle_share = own_slice(middle)
    normed_mid = norm_rows(middle, gain_mlp).astype(jnp.bfloat16)
    both = product(normed_mid, gu_flat).reshape(row_count, 2, hidden_units)
    gate_pre = both[:, 0]
    up_pre = both[:, 1]
    gate_sig = jax.nn.sigmoid(gate_pre)
    hidden = (gate_pre * gate_sig * up_pre).astype(jnp.bfloat16)
    down_share = lax.psum_scatter(
        product_t(hidden, down_full)
        .reshape(slot_count, half_rows, model_width)
        .astype(jnp.bfloat16),
        "tp",
        scatter_dimension=1,
        tiled=True,
    ).astype(jnp.float32)
    output = (valid_own * (middle_share + down_share)).astype(jnp.bfloat16)
    cot_rows = full_cot.reshape(row_count, model_width) * valid_rows.astype(jnp.bfloat16)
    d_hidden = product(cot_rows, down_full)
    d_gate = d_hidden * up_pre * gate_sig * (1.0 + gate_pre * (1.0 - gate_sig))
    d_up = d_hidden * gate_pre * gate_sig
    d_both = (
        jnp.stack([d_gate, d_up], axis=1).astype(jnp.bfloat16).reshape(row_count, 2 * hidden_units)
    )
    grad_down = outer_rows(cot_rows, hidden)
    grad_gu = outer_rows(normed_mid, d_both).reshape(model_width, 2, hidden_units)
    d_mid_terms = product_t(d_both, gu_flat)
    d_normed_mid = lax.psum(d_mid_terms, "tp")
    _, pull_mid = jax.vjp(norm_rows, middle, gain_mlp)
    d_middle_norm, d_gain_mlp_all = pull_mid(d_normed_mid)
    d_middle = d_middle_norm + cot_rows.astype(jnp.float32)
    feat_share = model_width // tensor_size
    owner = jnp.arange(model_width, dtype=jnp.int32) // feat_share == tensor_place
    d_gain_mlp_own = jnp.where(owner, d_gain_mlp_all, 0.0)
    d_branch = d_middle.astype(jnp.bfloat16)
    d_middle_share = own_slice(d_middle)
    d_gated = product(d_branch, out_full)
    grad_out = outer_rows(d_branch, gated)
    d_attended = (d_gated * opener).astype(jnp.bfloat16)
    d_open = (d_gated * attended_rows * opener * (1.0 - opener)).astype(jnp.bfloat16)
    grad_ogate = outer_rows(normed, d_open)
    da_items = by_head(d_attended.reshape(slot_count, half_rows, head_cols))

    def backward_item(pieces):
        query_block, key_block, value_block, cum_rows, cum_cols, lse_block, grad_block = pieces
        score_vals = score_block(query_block, key_block, cum_rows, cum_cols)
        attn_probs = jnp.exp(score_vals - lse_block[:, None])
        d_probs = product_t(grad_block, value_block)
        centre = jnp.sum(attn_probs * d_probs, axis=1, keepdims=True)
        d_scores = (attn_probs * (d_probs - centre)).astype(jnp.bfloat16)
        d_query_block = product(d_scores, key_block) * score_scale
        d_key_block = outer_rows(d_scores, query_block) * score_scale
        d_value_block = outer_rows(attn_probs.astype(jnp.bfloat16), grad_block)
        d_cum_rows = jnp.sum(d_scores, axis=1, dtype=jnp.float32)
        d_cum_cols = -jnp.sum(d_scores, axis=0, dtype=jnp.float32)
        return (d_query_block, d_key_block, d_value_block, d_cum_rows, d_cum_cols)

    dq_items, dk_items, dv_items, dcq_items, dck_items = lax.map(
        backward_item, (q_items, k_items, v_items, cq_items, ck_items, lse_items, da_items)
    )
    dc_own = dcq_items + dck_items[:, half_rows:]
    dc_left = dck_items[:, :half_rows]
    dc_left = dc_left.at[:, -1].add(jnp.sum(dc_own, axis=1))
    back_keys, back_values, back_cum = (
        shifted(to_slots(dk_items[:, :half_rows]).astype(jnp.bfloat16), "ctx", -1).astype(
            jnp.float32
        ),
        shifted(to_slots(dv_items[:, :half_rows]).astype(jnp.bfloat16), "ctx", -1).astype(
            jnp.float32
        ),
        shifted(to_slots_cum(dc_left).astype(jnp.bfloat16), "ctx", -1).astype(jnp.float32),
    )
    d_query = to_slots(dq_items).reshape(row_count, local_heads, head_size)
    d_key = (to_slots(dk_items[:, half_rows:]) + back_keys).reshape(
        row_count, local_heads, head_size
    )
    d_value = (to_slots(dv_items[:, half_rows:]) + back_values).reshape(row_count, head_cols)
    d_cum = to_slots_cum(dc_own) + back_cum
    d_log = jnp.flip(jnp.cumsum(jnp.flip(d_cum, 1), axis=1), 1)
    d_forget = d_log * jax.nn.sigmoid(-forget_pre)
    d_bias_own = jnp.sum(d_forget, axis=(0, 1))
    d_forget_low = d_forget.reshape(row_count, local_heads).astype(jnp.bfloat16)
    grad_forget = outer_rows(normed, d_forget_low)
    _, pull_query = jax.vjp(norm_rows, query_raw, qk_gain[0])
    d_query_raw, d_query_gain = pull_query(d_query)
    _, pull_key = jax.vjp(norm_rows, key_raw, qk_gain[1])
    d_key_raw, d_key_gain = pull_key(d_key)
    d_mixed = (
        jnp.stack(
            [
                d_query_raw.reshape(row_count, head_cols),
                d_key_raw.reshape(row_count, head_cols),
                d_value,
            ],
            axis=1,
        )
        .astype(jnp.bfloat16)
        .reshape(row_count, 3 * head_cols)
    )
    grad_qkv = outer_rows(normed, d_mixed).reshape(model_width, 3, head_cols)
    d_normed = (
        product_t(d_mixed, qkv_flat)
        + product_t(d_open, ogate_full)
        + product_t(d_forget_low, forget_full)
    )
    root = lax.rsqrt(jnp.mean(residual * residual, axis=1, keepdims=True) + epsilon)
    unit = residual * root
    d_unit = d_normed * gain_attn
    dot_part = (jnp.sum(d_unit * unit, axis=1) / model_width).reshape(slot_count, half_rows)
    d_unit_share, dot_full = (
        lax.psum_scatter(
            d_unit.reshape(slot_count, half_rows, model_width).astype(jnp.bfloat16),
            "tp",
            scatter_dimension=1,
            tiled=True,
        ).astype(jnp.float32),
        lax.psum_scatter(
            dot_part.astype(jnp.bfloat16), "tp", scatter_dimension=1, tiled=True
        ).astype(jnp.float32),
    )
    unit_share = own_slice(unit)
    root_share = own_slice(root)
    input_grad = (
        d_middle_share + root_share * (d_unit_share - unit_share * dot_full[:, :, None])
    ).astype(jnp.bfloat16)
    grad_parts = (
        lax.psum_scatter(
            grad_qkv.astype(jnp.bfloat16), ("shard", "ctx"), scatter_dimension=0, tiled=True
        ).astype(jnp.float32),
        lax.psum_scatter(
            grad_forget.astype(jnp.bfloat16), ("shard", "ctx"), scatter_dimension=0, tiled=True
        ).astype(jnp.float32),
        lax.psum_scatter(
            grad_ogate.astype(jnp.bfloat16), ("shard", "ctx"), scatter_dimension=0, tiled=True
        ).astype(jnp.float32),
        lax.psum_scatter(
            grad_out.astype(jnp.bfloat16), ("shard", "ctx"), scatter_dimension=0, tiled=True
        ).astype(jnp.float32),
        lax.psum_scatter(
            grad_gu.astype(jnp.bfloat16), ("shard", "ctx"), scatter_dimension=0, tiled=True
        ).astype(jnp.float32),
        lax.psum_scatter(
            grad_down.astype(jnp.bfloat16), ("shard", "ctx"), scatter_dimension=0, tiled=True
        ).astype(jnp.float32),
    )
    bias_full = lax.dynamic_update_slice_in_dim(
        jnp.zeros(forget_bias.shape, jnp.float32), d_bias_own, tensor_place * local_heads, 0
    )
    gain_attn_part = jnp.sum(d_normed * unit, axis=0)
    small_parts = lax.psum(
        (gain_attn_part, d_gain_mlp_own, jnp.stack([d_query_gain, d_key_gain]), bias_full),
        ("shard", "ctx", "tp"),
    )
    return (
        output,
        input_grad,
        grad_parts[0],
        grad_parts[1],
        small_parts[3],
        grad_parts[2],
        grad_parts[3],
        grad_parts[4],
        grad_parts[5],
        small_parts[0],
        small_parts[1],
        small_parts[2],
    )


def solution(mesh):
    return jax.shard_map(
        body,
        mesh=mesh,
        in_specs=(
            P("shard", ("ctx", "tp"), None),
            P("shard", ("ctx", "tp"), None),
            P("shard"),
            P(("shard", "ctx"), None, "tp"),
            P(("shard", "ctx"), "tp"),
            P(),
            P(("shard", "ctx"), "tp"),
            P(("shard", "ctx"), "tp"),
            P(("shard", "ctx"), None, "tp"),
            P(("shard", "ctx"), "tp"),
            P(),
            P(),
            P(),
        ),
        out_specs=(
            P("shard", ("ctx", "tp"), None),
            P("shard", ("ctx", "tp"), None),
            P(("shard", "ctx"), None, "tp"),
            P(("shard", "ctx"), "tp"),
            P(),
            P(("shard", "ctx"), "tp"),
            P(("shard", "ctx"), "tp"),
            P(("shard", "ctx"), None, "tp"),
            P(("shard", "ctx"), "tp"),
            P(),
            P(),
            P(),
        ),
        check_vma=False,
    )
```

profile of v0, /device:TPU:0, one launch (start us, length us, event | category | flops | bytes accessed | tf_op | source)
XLA Modules:
  0.0 1049.7 jit_solution(11627350117377922482)
XLA Ops:
  11.9 10.6 %all-gather = bf16[8,192,6]{1,2,0:T(8,128)(2,1)S(1)} all-gather(bf16[1,192,6]{1,2,0:T(8,128)(2,1)} %bitcast.510), channel_id=1, replica_groups=mesh['shard'=4,'ctx'=2,'tp'=4] {'shard','ctx'}, dimensions={0}, use_global_device_ids=true | all-gather | bytes 20736 | tf_op jit(solution)/shard_map/all_gather | solution.py:70
  24.6 24.8 %all-gather.9.cloned.1.call-done = bf16[1,512,1536]{2,1,0:T(8,128)(2,1)} async-done(((bf16[1,128,1536]{2,1,0:T(8,128)(2,1)}), bf16[1,512,1536]{2,1,0:T(8,128)(2,1)}) %all-gather.9.cloned.1.call-update) | async-done | bytes 1572880 | tf_op jit(solution)/shard_map/all_gather | solution.py:65
  59.5 24.7 %all-gather.11.cloned.1.call-done = bf16[1536,3,384]{2,0,1:T(8,128)(2,1)} async-done(((bf16[192,3,384]{2,0,1:T(8,128)(2,1)}), bf16[1536,3,384]{2,0,1:T(8,128)(2,1)}) %all-gather.11.cloned.1.call-update) | async-done | bytes 3538960 | tf_op jit(solution)/shard_map/all_gather | solution.py:69
  84.2 6.1 copy.92
  90.3 4.1 fusion.41
  118.7 37.0 %while.31 = (s32[]{:T(128)}, f32[6,512,64]{1,2,0:T(8,128)}, f32[6,512]{1,0:T(8,128)S(1)}, bf16[6,512,64]{2,1,0:T(8,128)(2,1)}, bf16[6,1024,64]{2,1,0:T(8,128)(2,...) while((s32[]{:T(128)}, f32[6,512,64]{1,2,0:T(8,128)}, ...), condition=%wide.region_8.9_spmd, body=%wide.region_5.8_spmd.sunk | while | flops 139460096 | bytes 7643265 | solution.py:151
  159.7 4.0 fusion.126
  168.9 116.0 %all-reduce.5.cloned.1.call-done = f32[512,1536]{1,0:T(8,128)} async-done(((f32[512,1536]{1,0:T(8,128)}), f32[512,1536]{1,0:T(8,128)}) %all-reduce.5.cloned.1.call-update) | async-done | bytes 3145744 | tf_op jit(solution)/shard_map/psum | solution.py:158
  289.3 42.5 %all-gather.17.cloned.1.call-done = bf16[1536,2,1024]{2,0,1:T(8,128)(2,1)} async-done(((bf16[192,2,1024]{2,0,1:T(8,128)(2,1)}), bf16[1536,2,1024]{2,0,1:T(8,128)(2,1)}) %all-gather.17.cloned.1.call-update) | async-done | bytes 6291472 | tf_op jit(solution)/shard_map/all_gather | solution.py:73
  331.8 8.7 copy.104
  340.5 8.1 fusion.36
  348.6 21.9 %all-gather.21.cloned.1.call-done = bf16[1,512,1536]{2,1,0:T(8,128)(2,1)} async-done(((bf16[1,128,1536]{2,1,0:T(8,128)(2,1)}), bf16[1,512,1536]{2,1,0:T(8,128)(2,1)}) %all-gather.21.cloned.1.call-update) | async-done | bytes 1572880 | tf_op jit(solution)/shard_map/all_gather | solution.py:66
  370.5 33.1 %all-gather.19.cloned.1.call-done = bf16[1536,1024]{1,0:T(8,128)(2,1)} async-done(((bf16[192,1024]{1,0:T(8,128)(2,1)}), bf16[1536,1024]{1,0:T(8,128)(2,1)}) %all-gather.19.cloned.1.call-update) | async-done | bytes 3145744 | tf_op jit(solution)/shard_map/all_gather | solution.py:74
  403.6 5.9 fusion.52
  410.9 8.0 convolution_bitcast_fusion.2
  423.5 6.7 fusion.47
  430.5 109.7 %all-reduce.7.cloned.1.call-done = f32[512,1536]{1,0:T(8,128)} async-done(((f32[512,1536]{1,0:T(8,128)}), f32[512,1536]{1,0:T(8,128)}) %all-reduce.7.cloned.1.call-update) | async-done | bytes 3145744 | tf_op jit(solution)/shard_map/psum | solution.py:186
  552.2 97.2 %while.32 = (s32[]{:T(128)}, f32[6,512,64]{1,2,0:T(8,128)}, f32[6,1024,64]{1,2,0:T(8,128)}, f32[6,1024,64]{1,2,0:T(8,128)}, f32[6,512]{1,0:T(8,128)}, /*index=5*...) while((s32[]{:T(128)}, f32[6,512,64]{1,2,0:T(8,128)}, ...), condition=%wide.region_18.19_spmd, body=%wide.region_14.18_spmd.sunk | while | flops 342981632 | bytes 20376776 | solution.py:216
  676.4 4.1 reduce-window.16
  711.4 3.4 multiply_reduce_fusion.2
  715.7 6.4 convolution_convert_fusion.2
  722.2 3.7 convolution_convert_fusion.5
  729.0 5.8 convolution_convert_fusion.1
  738.0 4.0 copy.114
  742.0 8.9 convolution_convert_fusion
  755.5 41.1 %all-reduce.1 = (f32[24]{0:T(128)}, f32[1536]{0:T(1024)}, f32[1536]{0:T(1024)}, f32[2,64]{1,0:T(2,128)}) all-reduce(f32[24]{0:T(128)S(1)} %dynamic_update_slice.28, f32[1536]{0:T(1024)S(1)} %get-tuple-element.207, f32[1536]{0:T(1024)S(1)} %fusion.108, ...), channel_id=1, replica_groups=mesh['shard'=4,'ctx'=2,'tp'=4] {'shard','ctx','tp'}, use_global_device_ids=true, to_apply=%region_30.31 | all-reduce | flops 3224 | bytes 25792 | tf_op jit(solution)/shard_map/psum | solution.py:308
  797.5 8.2 reduce-scatter.26.cloned.1.call-done
  807.7 37.9 %reduce-scatter.20.cloned.1.call-done = bf16[192,384]{1,0:T(8,128)(2,1)} async-done(((bf16[1536,384]{1,0:T(8,128)(2,1)}), bf16[192,384]{1,0:T(8,128)(2,1)}) %reduce-scatter.20.cloned.1.call-update) | async-done | bytes 147472 | tf_op jit(solution)/shard_map/reduce_scatter | solution.py:291
  847.2 38.6 %reduce-scatter.22.cloned.1.call-done = bf16[192,384]{1,0:T(8,128)(2,1)} async-done(((bf16[1536,384]{1,0:T(8,128)(2,1)}), bf16[192,384]{1,0:T(8,128)(2,1)}) %reduce-scatter.22.cloned.1.call-update) | async-done | bytes 147472 | tf_op jit(solution)/shard_map/reduce_scatter | solution.py:294
  887.5 36.4 %reduce-scatter.16.cloned.1.call-done = bf16[1,128,1536]{2,1,0:T(8,128)(2,1)} async-done(((bf16[1,512,1536]{2,1,0:T(8,128)(2,1)}), bf16[1,128,1536]{2,1,0:T(8,128)(2,1)}) %reduce-scatter.16.cloned.1.call-update) | async-done | bytes 393232 | tf_op jit(solution)/shard_map/reduce_scatter | solution.py:269
  926.1 48.2 %reduce-scatter.18.cloned.1.call-done = bf16[192,3,384]{2,0,1:T(8,128)(2,1)} async-done(((bf16[1536,3,384]{2,0,1:T(8,128)(2,1)}), bf16[192,3,384]{2,0,1:T(8,128)(2,1)}) %reduce-scatter.18.cloned.1.call-update) | async-done | bytes 442384 | tf_op jit(solution)/shard_map/reduce_scatter | solution.py:285
  976.3 63.0 %reduce-scatter.24.cloned.1.call-done = bf16[192,2,1024]{2,0,1:T(8,128)(2,1)} async-done(((bf16[1536,2,1024]{2,0,1:T(8,128)(2,1)}), bf16[192,2,1024]{2,0,1:T(8,128)(2,1)}) %reduce-scatter.24.cloned.1.call-update) | async-done | bytes 786448 | tf_op jit(solution)/shard_map/reduce_scatter | solution.py:297
  (435 shorter events, 288.3 us)
Async XLA Ops:
  7.2 17.4 %copy-start.69 = (f32[24]{0:T(128)S(1)}, f32[24]{0:T(128)}, u32[]{:S(2)}) copy-start(f32[24]{0:T(128)} %param.24) | copy-start | bytes 292
  7.2 42.2 %all-gather.9.cloned.1.call-start = ((), (), s32[]{:S(2)}) async-start(), calls=%async_computation.9 | async-start | bytes 1966080 | tf_op jit(solution)/shard_map/all_gather | solution.py:65
  7.9 76.3 %all-gather.11.cloned.1.call-start = ((), (), s32[]{:S(2)}) async-start(), calls=%async_computation.10 | async-start | bytes 3981312 | tf_op jit(solution)/shard_map/all_gather | solution.py:69
  8.7 42.5 %copy-start.59 = (f32[1536]{0:T(1024)S(1)}, f32[1536]{0:T(1024)}, u32[]{:S(2)}) copy-start(f32[1536]{0:T(1024)} %param.29) | copy-start | bytes 18436
  8.7 147.0 %all-gather.13.cloned.1.call-start = ((), (), s32[]{:S(2)}) async-start(), calls=%async_computation.11 | async-start | bytes 1327104 | tf_op jit(solution)/shard_map/all_gather | solution.py:71
  9.4 150.3 %all-gather.15.cloned.1.call-start = ((), (), s32[]{:S(2)}) async-start(), calls=%async_computation.12 | async-start | bytes 1327104 | tf_op jit(solution)/shard_map/all_gather | solution.py:72
  10.0 274.9 %all-reduce.5.cloned.1.call-start = ((), (), s32[]{:S(2)}) async-start(), calls=%async_computation.13 | async-start | bytes 6291456 | tf_op jit(solution)/shard_map/psum | solution.py:158
  11.5 84.3 %copy-start.49 = (f32[384]{0:T(512)}, f32[384]{0:T(512)S(1)}, u32[]{:S(2)}) copy-start(f32[384]{0:T(512)S(1)} %mul.513) | copy-start | bytes 4612
  22.7 30.5 %copy-start.39 = (bf16[1536,6]{0,1:T(8,128)(2,1)}, bf16[1536,6]{0,1:T(8,128)(2,1)S(1)}, u32[]{:S(2)}) copy-start(bf16[1536,6]{0,1:T(8,128)(2,1)S(1)} %reshape.771) | copy-start | bytes 55300
  51.2 39.1 %copy-start.57 = (f32[512]{0:T(512)}, f32[512]{0:T(512)S(1)}, u32[]{:S(2)}) copy-start(f32[512]{0:T(512)S(1)} %add_rsqrt_fusion) | copy-start | bytes 6148
  55.5 2.4 collective-permute-start.1
  59.5 30.8 %copy-start.2 = (bf16[1,512,1536]{2,1,0:T(8,128)(2,1)S(1)}, bf16[1,512,1536]{2,1,0:T(8,128)(2,1)}, u32[]{:S(2)}) copy-start(bf16[1,512,1536]{2,1,0:T(8,128)(2,1)} %all-gather.9.cloned.1.call-done) | copy-start | bytes 4718596
  94.6 9.4 copy-start.6
  96.7 13.4 %collective-permute-start = (bf16[1,512,384]{1,2,0:T(8,128)(2,1)}, bf16[1,512,384]{1,2,0:T(8,128)(2,1)}, u32[]{:S(2)}, u32[]{:S(2)}) collective-permute-start(bf16[1,512,384]{1,2,0:T(8,128)(2,1)} %multiply_convert_fusion.9), channel_id=1, source_target_pairs={{0,4},{1,5},{2,6},{3,7},{8,12},{9,13},{10,14},{11,15},{16,20},{17,... | collective-permute-start | bytes 1179656 | tf_op jit(solution)/shard_map/ppermute | solution.py:13
  99.6 12.7 %collective-permute-start.2 = (bf16[1,512,384]{1,2,0:T(8,128)(2,1)}, bf16[1,512,384]{1,2,0:T(8,128)(2,1)}, u32[]{:S(2)}, u32[]{:S(2)}) collective-permute-start(bf16[1,512,384]{1,2,0:T(8,128)(2,1)} %slice_bitcast_fusion.5), channel_id=1, source_target_pairs={{0,4},{1,5},{2,6},{3,7},{8,12},{9,13},{10,14},{11,15},{16,20},{17,... | collective-permute-start | bytes 1179656 | tf_op jit(solution)/shard_map/ppermute | solution.py:13
  163.7 168.1 %all-gather.17.cloned.1.call-start = ((), (), s32[]{:S(2)}) async-start(), calls=%async_computation.14 | async-start | bytes 7077888 | tf_op jit(solution)/shard_map/all_gather | solution.py:73
  165.9 204.6 %all-gather.21.cloned.1.call-start = ((), (), s32[]{:S(2)}) async-start(), calls=%async_computation.17 | async-start | bytes 1966080 | tf_op jit(solution)/shard_map/all_gather | solution.py:66
  166.7 236.9 %all-gather.19.cloned.1.call-start = ((), (), s32[]{:S(2)}) async-start(), calls=%async_computation.15 | async-start | bytes 3538944 | tf_op jit(solution)/shard_map/all_gather | solution.py:74
  167.4 372.7 %all-reduce.7.cloned.1.call-start = ((), (), s32[]{:S(2)}) async-start(), calls=%async_computation.18 | async-start | bytes 6291456 | tf_op jit(solution)/shard_map/psum | solution.py:186
  287.8 252.4 %copy-start = (f32[512,1536]{1,0:T(8,128)}, f32[512,1536]{1,0:T(8,128)S(1)}, u32[]{:S(2)}) copy-start(f32[512,1536]{1,0:T(8,128)S(1)} %get-tuple-element.267) | copy-start | bytes 9437188
  418.9 332.6 %reduce-scatter.14.cloned.1.call-start = ((), (), s32[]{:S(2)}) async-start(), calls=%async_computation.16 | async-start | bytes 1966080 | tf_op jit(solution)/shard_map/reduce_scatter | solution.py:167
  430.2 323.7 %reduce-scatter.30.cloned.1.call-start = ((), (), s32[]{:S(2)}) async-start(), calls=%async_computation.26 | async-start | bytes 442368
  653.4 51.8 %collective-permute-start.4 = (bf16[1,512,384]{1,2,0:T(8,128)(2,1)}, bf16[1,512,384]{1,2,0:T(8,128)(2,1)}, u32[]{:S(2)}, u32[]{:S(2)}) collective-permute-start(bf16[1,512,384]{1,2,0:T(8,128)(2,1)} %bitcast.100), channel_id=1, source_target_pairs={{4,0},{5,1},{6,2},{7,3},{12,8},{13,9},{14,10},{15,11},{20,16},{21,... | collective-permute-start | bytes 1179656 | tf_op jit(solution)/shard_map/ppermute | solution.py:13
  656.6 44.0 %collective-permute-start.3 = (bf16[1,512,384]{1,2,0:T(8,128)(2,1)}, bf16[1,512,384]{1,2,0:T(8,128)(2,1)}, u32[]{:S(2)}, u32[]{:S(2)}) collective-permute-start(bf16[1,512,384]{1,2,0:T(8,128)(2,1)} %bitcast.90), channel_id=1, source_target_pairs={{4,0},{5,1},{6,2},{7,3},{12,8},{13,9},{14,10},{15,11},{20,16},{21,... | collective-permute-start | bytes 1179656 | tf_op jit(solution)/shard_map/ppermute | solution.py:13
  665.8 6.0 collective-permute-start.5
  700.3 96.4 %reduce-scatter.28.cloned.1.call-start = ((), (), s32[]{:S(2)}) async-start(), calls=%async_computation.25 | async-start | bytes 163840
  715.7 90.0 %reduce-scatter.26.cloned.1.call-start = ((), (), s32[]{:S(2)}) async-start(), calls=%async_computation.24 | async-start | bytes 3538944 | tf_op jit(solution)/shard_map/reduce_scatter | solution.py:300
  722.2 123.4 %reduce-scatter.20.cloned.1.call-start = ((), (), s32[]{:S(2)}) async-start(), calls=%async_computation.21 | async-start | bytes 1327104 | tf_op jit(solution)/shard_map/reduce_scatter | solution.py:291
  725.9 159.9 %reduce-scatter.22.cloned.1.call-start = ((), (), s32[]{:S(2)}) async-start(), calls=%async_computation.22 | async-start | bytes 1327104 | tf_op jit(solution)/shard_map/reduce_scatter | solution.py:294
  728.0 195.8 %reduce-scatter.16.cloned.1.call-start = ((), (), s32[]{:S(2)}) async-start(), calls=%async_computation.19 | async-start | bytes 1966080 | tf_op jit(solution)/shard_map/reduce_scatter | solution.py:269
  728.6 245.7 %reduce-scatter.18.cloned.1.call-start = ((), (), s32[]{:S(2)}) async-start(), calls=%async_computation.20 | async-start | bytes 3981312 | tf_op jit(solution)/shard_map/reduce_scatter | solution.py:285
  734.9 304.4 %reduce-scatter.24.cloned.1.call-start = ((), (), s32[]{:S(2)}) async-start(), calls=%async_computation.23 | async-start | bytes 7077888 | tf_op jit(solution)/shard_map/reduce_scatter | solution.py:297
  (67 other events, 194.6 us)
Sparse Core Ops, SparseCore 0:
  9.6 39.7 all-gather.8
  51.3 32.8 all-gather.10
  86.1 24.0 all-gather.12
  112.0 24.0 all-gather.14
  163.8 121.0 all-reduce.4
  287.2 44.5 all-gather.16
  333.4 37.0 all-gather.20
  372.4 31.1 all-gather.18
  419.0 121.0 all-reduce.6
  542.3 34.2 reduce-scatter.13
  700.4 35.1 reduce-scatter.29
  738.2 19.1 reduce-scatter.27
  761.2 44.4 reduce-scatter.25
  808.8 36.7 reduce-scatter.19
  849.0 36.7 reduce-scatter.21
  888.6 35.2 reduce-scatter.15
  927.2 47.0 reduce-scatter.17
  977.5 61.7 reduce-scatter.23
where the time goes:
time: 1060 us; the launch traced here: 1050 us
  waiting for transfers between devices  611 us (58%)
  matrix products  162 us (15%)
  local copies, waits for them, and re-layouts  121 us (11%)
  other arithmetic  75.4 us (7%)
  blocking collectives  51.8 us (5%)
  between operations  16.4 us (2%)
  starting transfers between devices  12.2 us (1%)
    psum x1, waiting for transfers between devices, body(): branch_full = lax.psum(branch_part, 'tp')  116 us
    psum x1, waiting for transfers between devices, body(): d_normed_mid = lax.psum(d_mid_terms, 'tp')  110 us
    reduce_scatter x1, waiting for transfers between devices, body(): lax.psum_scatter(grad_gu.astype(jnp.bfloat16), ('shard', 'ctx'), scatter_...  63 us
    dot_general x24, matrix products, product_t(): lax.dot_general(left, right, (((1,), (1,)), ((), ())), preferred_element_...  58 us
    dot_general x18, matrix products, outer_rows(): lax.dot_general(left, right, (((0,), (0,)), ((), ())), preferred_element_...  52.8 us
    dot_general x18, matrix products, product(): return jnp.dot(left, right, preferred_element_type=jnp.float32)  51.2 us
    reduce_scatter x1, waiting for transfers between devices, body(): lax.psum_scatter(grad_qkv.astype(jnp.bfloat16), ('shard', 'ctx'), scatter...  48.2 us
    all_gather x1, waiting for transfers between devices, body(): lax.all_gather(w_gu, ('shard', 'ctx'), axis=0, tiled=True)  42.5 us
  transfers between devices with their start and end apart: 24, of which 14 were waited for; matrix products, arithmetic and copies ran while one was open for 31% of the time, Pallas kernels for 0%

commit v1 on v0

--- a/solution.py
+++ b/solution.py
@@ -5,6 +5,24 @@
 from jax.sharding import PartitionSpec as P
 
 epsilon = 1e-06
+
+
+def gather_around(value, axis, dim):
+    ways, here, lap = (lax.axis_size(axis), lax.axis_index(axis), value.shape[dim])
+    shape = [n * ways if d == dim else n for d, n in enumerate(value.shape)]
+    full = lax.dynamic_update_slice_in_dim(
+        jnp.zeros(shape, value.dtype), value, here * lap, axis=dim
+    )
+    going_up = going_down = value
+    for far in range(1, ways // 2 + 1):
+        going_up = lax.ppermute(going_up, axis, [(d, (d + 1) % ways) for d in range(ways)])
+        full = lax.dynamic_update_slice_in_dim(full, going_up, (here - far) % ways * lap, axis=dim)
+        if 2 * far < ways:
+            going_down = lax.ppermute(going_down, axis, [(d, (d - 1) % ways) for d in range(ways)])
+            full = lax.dynamic_update_slice_in_dim(
+                full, going_down, (here + far) % ways * lap, axis=dim
+            )
+    return full
 
 
 def shifted(block, axis, distance):
@@ -62,7 +80,7 @@
     score_scale = 1.0 / math.sqrt(head_size)
     own_start = tensor_place * own_rows
     full_tokens, full_cot = (
-        lax.all_gather(tokens, "tp", axis=1, tiled=True),
+        gather_around(tokens, "tp", 1),
         lax.all_gather(cotangent, "tp", axis=1, tiled=True),
     )
     qkv_full, forget_full, ogate_full, out_full, gu_full, down_full = (

time: 1060 us -> 1030 us (0.972)
  waiting for transfers between devices: 611 us -> 572 us
    all_gather x1 -> x0, waiting for transfers between devices: 24.8 us -> none  [body(): lax.all_gather(tokens, 'tp', axis=1, tiled=True)]
    all_gather x1, waiting for transfers between devices: 24.7 us -> 0.01 us  [body(): lax.all_gather(w_qkv, ('shard', 'ctx'), axis=0, tiled=True)]
    ppermute x0 -> x3, waiting for transfers between devices: none -> 13.1 us  [the longest x2 9.63 us: gather_around(): lax.ppermute(going_up, axis, [(d, (d + 1) % ways) for d in range(ways)])]
  transfers between devices with their start and end apart: 24 -> 26, of which waited for: 14 -> 14; matrix products, arithmetic and copies ran while one was open for 31% -> 32% of each run, Pallas kernels for 0% -> 0%
where the time goes in v1:
time: 1030 us; the launch traced here: 1010 us
  waiting for transfers between devices  572 us (56%)
  matrix products  161 us (16%)
  local copies, waits for them, and re-layouts  121 us (12%)
  other arithmetic  74 us (7%)
  blocking collectives  50.5 us (5%)
  starting transfers between devices  17.2 us (2%)
  between operations  15.8 us (2%)
    psum x1, waiting for transfers between devices, body(): branch_full = lax.psum(branch_part, 'tp')  115 us
    psum x1, waiting for transfers between devices, body(): d_normed_mid = lax.psum(d_mid_terms, 'tp')  110 us
    reduce_scatter x1, waiting for transfers between devices, body(): lax.psum_scatter(grad_gu.astype(jnp.bfloat16), ('shard', 'ctx'), scatter_...  63 us
    dot_general x24, matrix products, product_t(): lax.dot_general(left, right, (((1,), (1,)), ((), ())), preferred_element_...  58 us
    dot_general x18, matrix products, outer_rows(): lax.dot_general(left, right, (((0,), (0,)), ((), ())), preferred_element_...  52.9 us
    dot_general x18, matrix products, product(): return jnp.dot(left, right, preferred_element_type=jnp.float32)  49.8 us
    reduce_scatter x1, waiting for transfers between devices, body(): lax.psum_scatter(grad_qkv.astype(jnp.bfloat16), ('shard', 'ctx'), scatter...  48.2 us
    all_gather x1, waiting for transfers between devices, body(): lax.all_gather(w_gu, ('shard', 'ctx'), axis=0, tiled=True)  42.5 us
  transfers between devices with their start and end apart: 26, of which 14 were waited for; matrix products, arithmetic and copies ran while one was open for 32% of the time, Pallas kernels for 0%

profile of v1, /device:TPU:0, one launch (start us, length us, event | category | flops | bytes accessed | tf_op | source)
XLA Modules:
  0.0 1011.7 jit_solution(4696590939573946795)
XLA Ops:
  15.9 9.4 all-gather
  31.0 9.6 collective-permute-done.2
  47.7 6.0 copy.92
  53.7 4.2 fusion.38
  82.2 36.9 %while.31 = (s32[]{:T(128)}, f32[6,512,64]{1,2,0:T(8,128)}, f32[6,512]{1,0:T(8,128)S(1)}, bf16[6,512,64]{2,1,0:T(8,128)(2,1)}, bf16[6,1024,64]{2,1,0:T(8,128)(2,...) while((s32[]{:T(128)}, f32[6,512,64]{1,2,0:T(8,128)}, ...), condition=%wide.region_8.9_spmd, body=%wide.region_5.8_spmd.sunk | while | flops 139460096 | bytes 7643265 | solution.py:169
  119.8 3.5 fusion.78
  123.2 4.0 fusion.116
  132.1 115.3 %all-reduce.5.cloned.1.call-done = f32[512,1536]{1,0:T(8,128)} async-done(((f32[512,1536]{1,0:T(8,128)}), f32[512,1536]{1,0:T(8,128)}) %all-reduce.5.cloned.1.call-update) | async-done | bytes 3145744 | tf_op jit(solution)/shard_map/psum | solution.py:176
  251.7 42.5 %all-gather.14.cloned.1.call-done = bf16[1536,2,1024]{2,0,1:T(8,128)(2,1)} async-done(((bf16[192,2,1024]{2,0,1:T(8,128)(2,1)}), bf16[1536,2,1024]{2,0,1:T(8,128)(2,1)}) %all-gather.14.cloned.1.call-update) | async-done | bytes 6291472 | tf_op jit(solution)/shard_map/all_gather | solution.py:91
  294.2 8.7 copy.104
  302.9 8.0 fusion.36
  310.9 21.8 %all-gather.18.cloned.1.call-done = bf16[1,512,1536]{2,1,0:T(8,128)(2,1)} async-done(((bf16[1,128,1536]{2,1,0:T(8,128)(2,1)}), bf16[1,512,1536]{2,1,0:T(8,128)(2,1)}) %all-gather.18.cloned.1.call-update) | async-done | bytes 1572880 | tf_op jit(solution)/shard_map/all_gather | solution.py:84
  332.8 33.1 %all-gather.16.cloned.1.call-done = bf16[1536,1024]{1,0:T(8,128)(2,1)} async-done(((bf16[192,1024]{1,0:T(8,128)(2,1)}), bf16[1536,1024]{1,0:T(8,128)(2,1)}) %all-gather.16.cloned.1.call-update) | async-done | bytes 3145744 | tf_op jit(solution)/shard_map/all_gather | solution.py:92
  365.8 5.9 fusion.47
  373.1 8.0 convolution_bitcast_fusion.2
  385.8 6.7 fusion.42
  392.8 109.6 %all-reduce.7.cloned.1.call-done = f32[512,1536]{1,0:T(8,128)} async-done(((f32[512,1536]{1,0:T(8,128)}), f32[512,1536]{1,0:T(8,128)}) %all-reduce.7.cloned.1.call-update) | async-done | bytes 3145744 | tf_op jit(solution)/shard_map/psum | solution.py:204
  514.5 97.3 %while.32 = (s32[]{:T(128)}, f32[6,512,64]{1,2,0:T(8,128)}, f32[6,1024,64]{1,2,0:T(8,128)}, f32[6,1024,64]{1,2,0:T(8,128)}, f32[6,512]{1,0:T(8,128)}, /*index=5*...) while((s32[]{:T(128)}, f32[6,512,64]{1,2,0:T(8,128)}, ...), condition=%wide.region_18.19_spmd, body=%wide.region_14.18_spmd.sunk | while | flops 342981632 | bytes 20376776 | solution.py:234
  638.9 4.1 reduce-window.16
  673.9 3.4 multiply_reduce_fusion.2
  678.3 6.4 convolution_convert_fusion.2
  684.7 3.7 convolution_convert_fusion.5
  691.6 5.8 convolution_convert_fusion.1
  700.6 4.0 copy.114
  704.5 8.8 convolution_convert_fusion
  718.1 41.2 %all-reduce.1 = (f32[24]{0:T(128)}, f32[1536]{0:T(1024)}, f32[1536]{0:T(1024)}, f32[2,64]{1,0:T(2,128)}) all-reduce(f32[24]{0:T(128)S(1)} %dynamic_update_slice.48, f32[1536]{0:T(1024)S(1)} %get-tuple-element.207, f32[1536]{0:T(1024)S(1)} %fusion.102, ...), channel_id=1, replica_groups=mesh['shard'=4,'ctx'=2,'tp'=4] {'shard','ctx','tp'}, use_global_device_ids=true, to_apply=%region_30.31 | all-reduce | flops 3224 | bytes 25792 | tf_op jit(solution)/shard_map/psum | solution.py:326
  760.0 8.2 reduce-scatter.26.cloned.1.call-done
  770.2 38.1 %reduce-scatter.20.cloned.1.call-done = bf16[192,384]{1,0:T(8,128)(2,1)} async-done(((bf16[1536,384]{1,0:T(8,128)(2,1)}), bf16[192,384]{1,0:T(8,128)(2,1)}) %reduce-scatter.20.cloned.1.call-update) | async-done | bytes 147472 | tf_op jit(solution)/shard_map/reduce_scatter | solution.py:309
  809.9 38.6 %reduce-scatter.22.cloned.1.call-done = bf16[192,384]{1,0:T(8,128)(2,1)} async-done(((bf16[1536,384]{1,0:T(8,128)(2,1)}), bf16[192,384]{1,0:T(8,128)(2,1)}) %reduce-scatter.22.cloned.1.call-update) | async-done | bytes 147472 | tf_op jit(solution)/shard_map/reduce_scatter | solution.py:312
  850.1 36.4 %reduce-scatter.16.cloned.1.call-done = bf16[1,128,1536]{2,1,0:T(8,128)(2,1)} async-done(((bf16[1,512,1536]{2,1,0:T(8,128)(2,1)}), bf16[1,128,1536]{2,1,0:T(8,128)(2,1)}) %reduce-scatter.16.cloned.1.call-update) | async-done | bytes 393232 | tf_op jit(solution)/shard_map/reduce_scatter | solution.py:287
  888.7 48.2 %reduce-scatter.18.cloned.1.call-done = bf16[192,3,384]{2,0,1:T(8,128)(2,1)} async-done(((bf16[1536,3,384]{2,0,1:T(8,128)(2,1)}), bf16[192,3,384]{2,0,1:T(8,128)(2,1)}) %reduce-scatter.18.cloned.1.call-update) | async-done | bytes 442384 | tf_op jit(solution)/shard_map/reduce_scatter | solution.py:303
  938.9 63.0 %reduce-scatter.24.cloned.1.call-done = bf16[192,2,1024]{2,0,1:T(8,128)(2,1)} async-done(((bf16[1536,2,1024]{2,0,1:T(8,128)(2,1)}), bf16[192,2,1024]{2,0,1:T(8,128)(2,1)}) %reduce-scatter.24.cloned.1.call-update) | async-done | bytes 786448 | tf_op jit(solution)/shard_map/reduce_scatter | solution.py:315
  (445 shorter events, 289.4 us)
Async XLA Ops:
  7.2 20.1 %copy-start.70 = (f32[24]{0:T(128)S(1)}, f32[24]{0:T(128)}, u32[]{:S(2)}) copy-start(f32[24]{0:T(128)} %param.24) | copy-start | bytes 292
  7.2 40.5 %all-gather.8.cloned.1.call-start = ((), (), s32[]{:S(2)}) async-start(), calls=%async_computation.9 | async-start | bytes 3981312 | tf_op jit(solution)/shard_map/all_gather | solution.py:87
  7.9 19.5 %copy-start.30 = (bf16[1,128,1536]{2,1,0:T(8,128)(2,1)S(1)}, bf16[1,128,1536]{2,1,0:T(8,128)(2,1)}, u32[]{:S(2)}) copy-start(bf16[1,128,1536]{2,1,0:T(8,128)(2,1)} %param.19) | copy-start | bytes 1179652
  7.9 111.3 %all-gather.10.cloned.1.call-start = ((), (), s32[]{:S(2)}) async-start(), calls=%async_computation.10 | async-start | bytes 1327104 | tf_op jit(solution)/shard_map/all_gather | solution.py:89
  8.7 114.5 %all-gather.12.cloned.1.call-start = ((), (), s32[]{:S(2)}) async-start(), calls=%async_computation.11 | async-start | bytes 1327104 | tf_op jit(solution)/shard_map/all_gather | solution.py:90
  8.7 18.8 %collective-permute-start = (bf16[1,128,1536]{2,1,0:T(8,128)(2,1)}, bf16[1,128,1536]{2,1,0:T(8,128)(2,1)S(1)}, u32[]{:S(2)}, u32[]{:S(2)}) collective-permute-start(bf16[1,128,1536]{2,1,0:T(8,128)(2,1)} %param.19), channel_id=1, source_target_pairs={{0,1},{1,2},{2,3},{3,0},{4,5},{5,6},{6,7},{7,4},{8,9},{9,10},{10,1... | collective-permute-start | bytes 1179656 | tf_op jit(solution)/shard_map/ppermute | solution.py:18
  11.8 19.2 %collective-permute-start.1 = (bf16[1,128,1536]{2,1,0:T(8,128)(2,1)}, bf16[1,128,1536]{2,1,0:T(8,128)(2,1)S(1)}, u32[]{:S(2)}, u32[]{:S(2)}) collective-permute-start(bf16[1,128,1536]{2,1,0:T(8,128)(2,1)} %param.19), channel_id=1, source_target_pairs={{0,3},{1,0},{2,1},{3,2},{4,7},{5,4},{6,5},{7,6},{8,11},{9,8},{10,9... | collective-permute-start | bytes 1179656 | tf_op jit(solution)/shard_map/ppermute | solution.py:21
  13.9 233.4 %all-reduce.5.cloned.1.call-start = ((), (), s32[]{:S(2)}) async-start(), calls=%async_computation.12 | async-start | bytes 6291456 | tf_op jit(solution)/shard_map/psum | solution.py:176
  15.9 43.4 %copy-start.50 = (f32[384]{0:T(512)}, f32[384]{0:T(512)S(1)}, u32[]{:S(2)}) copy-start(f32[384]{0:T(512)S(1)} %mul.512) | copy-start | bytes 4612
  25.4 15.8 %copy-start.40 = (bf16[1536,6]{0,1:T(8,128)(2,1)}, bf16[1536,6]{0,1:T(8,128)(2,1)S(1)}, u32[]{:S(2)}) copy-start(bf16[1536,6]{0,1:T(8,128)(2,1)S(1)} %reshape.750) | copy-start | bytes 55300
  27.5 13.2 %collective-permute-start.2 = (bf16[1,128,1536]{2,1,0:T(8,128)(2,1)S(1)}, bf16[1,128,1536]{2,1,0:T(8,128)(2,1)S(1)}, u32[]{:S(2)}, u32[]{:S(2)}) collective-permute-start(bf16[1,128,1536]{2,1,0:T(8,128)(2,1)S(1)} %collective-permute-done), channel_id=1, source_target_pairs={{0,1},{1,2},{2,3},{3,0},{4,5},{5,6},{6,7},{7,4},{8,9},{9,10},{10,1... | collective-permute-start | bytes 1179656 | tf_op jit(solution)/shard_map/ppermute | solution.py:18
  40.7 79.0 %copy-start.1 = (bf16[512,1536]{1,0:T(8,128)(2,1)}, bf16[512,1536]{1,0:T(8,128)(2,1)S(1)}, u32[]{:S(2)}) copy-start(bf16[512,1536]{1,0:T(8,128)(2,1)S(1)} %bitcast_dynamic-update-slice_fusion) | copy-start | bytes 4718596
  44.0 2.1 collective-permute-start.4
  60.2 13.5 %collective-permute-start.3 = (bf16[1,512,384]{1,2,0:T(8,128)(2,1)}, bf16[1,512,384]{1,2,0:T(8,128)(2,1)}, u32[]{:S(2)}, u32[]{:S(2)}) collective-permute-start(bf16[1,512,384]{1,2,0:T(8,128)(2,1)} %multiply_convert_fusion.9), channel_id=1, source_target_pairs={{0,4},{1,5},{2,6},{3,7},{8,12},{9,13},{10,14},{11,15},{16,20},{17,... | collective-permute-start | bytes 1179656 | tf_op jit(solution)/shard_map/ppermute | solution.py:31
  63.1 12.6 %collective-permute-start.5 = (bf16[1,512,384]{1,2,0:T(8,128)(2,1)}, bf16[1,512,384]{1,2,0:T(8,128)(2,1)}, u32[]{:S(2)}, u32[]{:S(2)}) collective-permute-start(bf16[1,512,384]{1,2,0:T(8,128)(2,1)} %slice_bitcast_fusion.5), channel_id=1, source_target_pairs={{0,4},{1,5},{2,6},{3,7},{8,12},{9,13},{10,14},{11,15},{16,20},{17,... | collective-permute-start | bytes 1179656 | tf_op jit(solution)/shard_map/ppermute | solution.py:31
  127.2 167.0 %all-gather.14.cloned.1.call-start = ((), (), s32[]{:S(2)}) async-start(), calls=%async_computation.13 | async-start | bytes 7077888 | tf_op jit(solution)/shard_map/all_gather | solution.py:91
  129.5 203.3 %all-gather.18.cloned.1.call-start = ((), (), s32[]{:S(2)}) async-start(), calls=%async_computation.16 | async-start | bytes 1966080 | tf_op jit(solution)/shard_map/all_gather | solution.py:84
  130.0 235.8 %all-gather.16.cloned.1.call-start = ((), (), s32[]{:S(2)}) async-start(), calls=%async_computation.14 | async-start | bytes 3538944 | tf_op jit(solution)/shard_map/all_gather | solution.py:92
  130.8 371.6 %all-reduce.7.cloned.1.call-start = ((), (), s32[]{:S(2)}) async-start(), calls=%async_computation.17 | async-start | bytes 6291456 | tf_op jit(solution)/shard_map/psum | solution.py:204
  250.2 252.2 %copy-start = (f32[512,1536]{1,0:T(8,128)}, f32[512,1536]{1,0:T(8,128)S(1)}, u32[]{:S(2)}) copy-start(f32[512,1536]{1,0:T(8,128)S(1)} %get-tuple-element.267) | copy-start | bytes 9437188
  381.2 332.9 %reduce-scatter.14.cloned.1.call-start = ((), (), s32[]{:S(2)}) async-start(), calls=%async_computation.15 | async-start | bytes 1966080 | tf_op jit(solution)/shard_map/reduce_scatter | solution.py:185
  392.5 323.9 %reduce-scatter.30.cloned.1.call-start = ((), (), s32[]{:S(2)}) async-start(), calls=%async_computation.25 | async-start | bytes 442368
  615.8 52.0 %collective-permute-start.7 = (bf16[1,512,384]{1,2,0:T(8,128)(2,1)}, bf16[1,512,384]{1,2,0:T(8,128)(2,1)}, u32[]{:S(2)}, u32[]{:S(2)}) collective-permute-start(bf16[1,512,384]{1,2,0:T(8,128)(2,1)} %bitcast.102), channel_id=1, source_target_pairs={{4,0},{5,1},{6,2},{7,3},{12,8},{13,9},{14,10},{15,11},{20,16},{21,... | collective-permute-start | bytes 1179656 | tf_op jit(solution)/shard_map/ppermute | solution.py:31
  619.0 44.1 %collective-permute-start.6 = (bf16[1,512,384]{1,2,0:T(8,128)(2,1)}, bf16[1,512,384]{1,2,0:T(8,128)(2,1)}, u32[]{:S(2)}, u32[]{:S(2)}) collective-permute-start(bf16[1,512,384]{1,2,0:T(8,128)(2,1)} %bitcast.92), channel_id=1, source_target_pairs={{4,0},{5,1},{6,2},{7,3},{12,8},{13,9},{14,10},{15,11},{20,16},{21,... | collective-permute-start | bytes 1179656 | tf_op jit(solution)/shard_map/ppermute | solution.py:31
  628.1 6.1 collective-permute-start.8
  662.7 96.6 %reduce-scatter.28.cloned.1.call-start = ((), (), s32[]{:S(2)}) async-start(), calls=%async_computation.24 | async-start | bytes 163840
  678.2 90.0 %reduce-scatter.26.cloned.1.call-start = ((), (), s32[]{:S(2)}) async-start(), calls=%async_computation.23 | async-start | bytes 3538944 | tf_op jit(solution)/shard_map/reduce_scatter | solution.py:318
  684.7 123.6 %reduce-scatter.20.cloned.1.call-start = ((), (), s32[]{:S(2)}) async-start(), calls=%async_computation.20 | async-start | bytes 1327104 | tf_op jit(solution)/shard_map/reduce_scatter | solution.py:309
  688.4 160.0 %reduce-scatter.22.cloned.1.call-start = ((), (), s32[]{:S(2)}) async-start(), calls=%async_computation.21 | async-start | bytes 1327104 | tf_op jit(solution)/shard_map/reduce_scatter | solution.py:312
  690.6 195.9 %reduce-scatter.16.cloned.1.call-start = ((), (), s32[]{:S(2)}) async-start(), calls=%async_computation.18 | async-start | bytes 1966080 | tf_op jit(solution)/shard_map/reduce_scatter | solution.py:287
  691.2 245.8 %reduce-scatter.18.cloned.1.call-start = ((), (), s32[]{:S(2)}) async-start(), calls=%async_computation.19 | async-start | bytes 3981312 | tf_op jit(solution)/shard_map/reduce_scatter | solution.py:303
  697.4 304.5 %reduce-scatter.24.cloned.1.call-start = ((), (), s32[]{:S(2)}) async-start(), calls=%async_computation.22 | async-start | bytes 7077888 | tf_op jit(solution)/shard_map/reduce_scatter | solution.py:315
  (70 other events, 237.8 us)
Sparse Core Ops, SparseCore 0:
  9.9 36.6 all-gather.7
  48.5 24.0 all-gather.9
  74.5 24.0 all-gather.11
  127.4 119.9 all-reduce.4
  249.6 44.5 all-gather.13
  295.6 37.0 all-gather.17
  334.6 31.1 all-gather.15
  381.3 121.0 all-reduce.6
  504.7 34.2 reduce-scatter.13
  662.8 35.1 reduce-scatter.29
  700.8 19.2 reduce-scatter.27
  723.7 44.4 reduce-scatter.25
  771.4 36.7 reduce-scatter.19
  811.7 36.7 reduce-scatter.21
  851.2 35.2 reduce-scatter.15
  889.9 47.0 reduce-scatter.17
  940.2 61.7 reduce-scatter.23
